TPU v7x, 256 devices: a whole 4x4x8 slice. The times are simulated.
256 devices in a mesh: rows: 32 (over z, y), tab: 8 (over x, core).
Axes of the slice: x: 4, y: 4, z: 8, core: 2. Of those that a mesh axis runs over, the one named last changes fastest.
Arguments:
- vectors: bfloat16 [262144, 768], P(('rows', 'tab')), may hold values from -6 to 6
- list_owner: int32 [262144, 1], P(('rows', 'tab')), may hold values from 0 to 255; in each aligned block of 1024 rows (0 to 1023, 1024 to 2047, ...) at most 8 rows name the same one
- list_slot: int32 [262144], P(('rows', 'tab')), may hold values from 0 to 2047
- codes: int32 [262144, 96], P(('rows', 'tab')), may hold values from 0 to 255
- centroids: bfloat16 [524288, 768], P(('rows', 'tab')), may hold values from -6 to 6
- rotation: bfloat16 [768, 768], replicated, may hold values from -0.21875 to 0.21875
- old_codebooks: float32 [96, 8, 256], P('rows'), may hold values from -6 to 6
Outputs:
- codebooks: float32 [96, 8, 256], P('rows')
Inputs may be any that keep to these rules, and one draw needn't show every extreme that they name: `list_owner`: among the rows of one device, at most 8 rows name the same value, and in every draw some device has exactly 8 rows naming one value.
All inputs are finite; a program needn't handle non-finite values.
Results may differ from a plain program's by a relative error of at most 0.0015.
Values may be sent and summed in bfloat16 or wider, within the bound.
A program may use at most 64 MiB of HBM per device.

v0:
```python
import math

import jax
import jax.numpy as jnp
from jax import lax
from jax.sharding import PartitionSpec as P


def codeword_sums(parts, labels, codewords, block_rows):
    total_rows, sub_count, sub_width = parts.shape

    def accumulate(totals, offset):
        pieces = lax.dynamic_slice_in_dim(parts, offset, block_rows, 0)
        code_block = lax.dynamic_slice_in_dim(labels, offset, block_rows, 0)
        one_hot = (
            code_block[:, :, None] == jnp.arange(codewords, dtype=jnp.int32)[None, None, :]
        ).astype(jnp.bfloat16)
        added = jnp.einsum("bms,bmk->msk", pieces, one_hot, preferred_element_type=jnp.float32)
        tallies = jnp.sum(one_hot, axis=0, dtype=jnp.float32)
        return ((totals[0] + added, totals[1] + tallies), None)

    starts = jnp.arange(total_rows // block_rows, dtype=jnp.int32) * block_rows
    start_sums = jnp.zeros((sub_count, sub_width, codewords), jnp.float32)
    start_counts = jnp.zeros((sub_count, codewords), jnp.float32)
    result, _ = lax.scan(accumulate, (start_sums, start_counts), starts)
    return result


def body(vectors, list_owner, list_slot, codes, centroids, rotation, old_codebooks):
    n_rows = lax.axis_size("rows")
    n_tab = lax.axis_size("tab")
    devices = n_rows * n_tab
    row_dev, width = vectors.shape
    own_subspaces, sub_width, codewords = old_codebooks.shape
    subspaces = own_subspaces * n_rows
    capacity = 2 * row_dev // devices
    owners = list_owner[:, 0]
    owner_marks = (owners[:, None] == jnp.arange(devices, dtype=jnp.int32)[None, :]).astype(
        jnp.int32
    )
    running = jnp.cumsum(owner_marks, axis=0)
    position = jnp.sum(running * owner_marks, axis=1) - 1
    places = owners * capacity + position
    wanted = jnp.zeros((devices * capacity,), jnp.int32).at[places].set(list_slot)
    wanted = wanted.reshape(n_rows, n_tab, capacity)
    data_rot = jnp.dot(vectors, rotation, preferred_element_type=jnp.float32).astype(jnp.bfloat16)
    incoming = lax.all_to_all(
        lax.all_to_all(wanted, "rows", split_axis=0, concat_axis=0, tiled=True),
        "tab",
        split_axis=1,
        concat_axis=1,
        tiled=True,
    )
    answers = centroids[incoming]
    returned = lax.all_to_all(
        lax.all_to_all(answers, "rows", split_axis=0, concat_axis=0, tiled=True),
        "tab",
        split_axis=1,
        concat_axis=1,
        tiled=True,
    )
    fetched = returned.reshape(devices * capacity, width)[places]
    centre_rot = jnp.dot(fetched, rotation, preferred_element_type=jnp.float32).astype(jnp.bfloat16)
    centre_sums, unused_counts = codeword_sums(
        centre_rot.reshape(row_dev, subspaces, sub_width), codes, codewords, math.gcd(row_dev, 512)
    )
    total_rows = n_rows * row_dev
    block_rows = math.gcd(total_rows, 8192)
    code_parts = codes.reshape(row_dev, n_rows, own_subspaces)
    data_parts = data_rot.reshape(row_dev, n_rows, own_subspaces * sub_width)
    got_data, got_codes = (
        lax.all_to_all(data_parts, "rows", split_axis=1, concat_axis=0, tiled=True),
        lax.all_to_all(code_parts, "rows", split_axis=1, concat_axis=0, tiled=True),
    )
    got_codes = got_codes.reshape(total_rows, own_subspaces)
    word_sums, word_counts = codeword_sums(
        got_data.reshape(total_rows, own_subspaces, sub_width), got_codes, codewords, block_rows
    )
    word_sums = word_sums - lax.psum_scatter(
        centre_sums.astype(jnp.bfloat16), "rows", scatter_dimension=0, tiled=True
    ).astype(jnp.float32)
    word_sums, word_counts = lax.psum((word_sums, word_counts), "tab")
    prior_weight = float(row_dev * devices // codewords)
    return (word_sums + prior_weight * old_codebooks) / (word_counts[:, None, :] + prior_weight)


def solution(mesh):
    return jax.shard_map(
        body,
        mesh=mesh,
        in_specs=(
            P(("rows", "tab"), None),
            P(("rows", "tab"), None),
            P(("rows", "tab")),
            P(("rows", "tab"), None),
            P(("rows", "tab"), None),
            P(),
            P("rows", None, None),
        ),
        out_specs=P("rows", None, None),
        check_vma=False,
    )
```

profile of v0, /device:TPU:1, one launch (start us, length us, event | category | flops | bytes accessed | tf_op | source)
XLA Modules:
  0.0 512.5 jit_solution(5868722460316664837)
XLA Ops:
  15.7 21.2 %all_to_all.50 = s32[32,8,8]{2,1,0:T(8,128)S(1)} all-to-all(s32[32,8,8]{2,1,0:T(8,128)S(1)} %reshape.57), channel_id=1, replica_groups=mesh['rows'=32,'tab'=8] {'rows'}, dimensions={0} | all-to-all | bytes 16384 | tf_op jit(solution)/shard_map/all_to_all | solution.py:48
  37.0 10.8 %all_to_all.51 = s32[8,1,256]{2,1,0:T(1,128)S(1)} all-to-all(s32[8,1,256]{2,1,0:T(1,128)S(1)} %reshape.88), channel_id=1, replica_groups=mesh['rows'=32,'tab'=8] {'tab'}, dimensions={0} | all-to-all | bytes 16384 | tf_op jit(solution)/shard_map/all_to_all | solution.py:47
  49.3 9.4 %gather_fusion = bf16[2048,768]{1,0:T(8,128)(2,1)} fusion(bf16[2048,768]{1,0:T(8,128)(2,1)S(1)} %copy-done, s32[2048]{0:T(1024)S(1)} %broadcast_clamp_fusion), kind=kCustom, calls=%fused_computation | custom fusion | bytes 6299648 | tf_op jit(solution)/shard_map/gather | solution.py:54
  58.8 4.8 all-to-all-start.4
  68.0 66.7 %all-to-all-done.4 = bf16[32,8,8,768]{3,2,1,0:T(8,128)(2,1)} async-done(((bf16[32,8,8,768]{3,2,1,0:T(8,128)(2,1)}), bf16[32,8,8,768]{3,2,1,0:T(8,128)(2,1)}, u32[]{:S(2)}, u32[]{:S(2)}) %all-to-all-start.4) | async-done | bytes 3145760 | tf_op jit(solution)/shard_map/all_to_all | solution.py:56
  134.7 7.5 %all-to-all-start = ((bf16[1024,32,24]{0,2,1:T(8,128)(2,1)}), bf16[1024,32,24]{0,2,1:T(8,128)(2,1)}, u32[]{:S(2)}, u32[]{:S(2)}) async-start(bf16[1024,32,24]{0,2,1:T(8,128)(2,1)} %bitcast.46), calls=%async_computation | async-start | bytes 3145728 | tf_op jit(solution)/shard_map/all_to_all | solution.py:72
  146.0 34.0 %all-to-all-done = bf16[1024,32,24]{0,2,1:T(8,128)(2,1)} async-done(((bf16[1024,32,24]{0,2,1:T(8,128)(2,1)}), bf16[1024,32,24]{0,2,1:T(8,128)(2,1)}, u32[]{:S(2)}, u32[]{:S(2)}) %all-to-all-start) | async-done | bytes 1572896 | tf_op jit(solution)/shard_map/all_to_all | solution.py:72
  180.0 6.6 %all-to-all-start.5 = ((bf16[32,8,8,768]{3,2,0,1:T(8,128)(2,1)}), bf16[32,8,8,768]{3,2,0,1:T(8,128)(2,1)}, u32[]{:S(2)}, u32[]{:S(2)}) async-start(bf16[32,8,8,768]{3,2,0,1:T(8,128)(2,1)} %copy.26), calls=%async_computation.5 | async-start | bytes 6291456 | tf_op jit(solution)/shard_map/all_to_all | solution.py:55
  195.8 28.4 %all-to-all-done.5 = bf16[32,8,8,768]{3,2,0,1:T(8,128)(2,1)} async-done(((bf16[32,8,8,768]{3,2,0,1:T(8,128)(2,1)}), bf16[32,8,8,768]{3,2,0,1:T(8,128)(2,1)}, u32[]{:S(2)}, u32[]{:S(2)}) %all-to-all-start.5) | async-done | bytes 3145760 | tf_op jit(solution)/shard_map/all_to_all | solution.py:55
  224.1 5.6 %all-to-all-start.1 = ((s32[1024,32,3]{0,2,1:T(4,128)}), s32[1024,32,3]{0,2,1:T(4,128)}, u32[]{:S(2)}, u32[]{:S(2)}) async-start(s32[1024,32,3]{0,2,1:T(4,128)} %reshape.54), calls=%async_computation.1 | async-start | bytes 1048576 | tf_op jit(solution)/shard_map/all_to_all | solution.py:73
  234.0 7.9 %gather_fusion.1 = bf16[1024,768]{1,0:T(8,128)(2,1)} fusion(bf16[2048,768]{1,0:T(8,128)(2,1)} %bitcast.44, s32[1024]{0:T(1024)S(1)} %broadcast_clamp_fusion.1), kind=kCustom, calls=%fused_computation.1 | custom fusion | bytes 3149824 | tf_op jit(solution)/shard_map/gather | solution.py:62
  246.2 31.0 %while.25 = (s32[]{:T(128)}, f32[96,8,256]{2,1,0:T(8,128)}, s32[2]{0:T(128)S(1)}, bf16[1024,96,8]{0,2,1:T(8,128)(2,1)}, s32[1024,96]{0,1:T(8,128)}, /*index=5*/s32[]{:T(128)}, s32[]{:T(128)}, s32[]{:T(128)}) while((s32[]{:T(128)}, f32[96,8,256]{2,1,0:T(8,128)}, s32[2]{0:T(128)S(1)}, bf16[1024,96,8]{0,2,1:T(8,128)(2,1)}, ...), condition=%wide.region_8.9_spmd.clone, body=%wide.region_7.8_spmd.clone.sunk | while | flops 214302720 | bytes 2949269 | solution.py:25
  249.5 12.2 %fusion.32 = f32[96,8,256]{2,1,0:T(8,128)} fusion(s32[512,96]{0,1:T(8,128)S(1)} %constant_dynamic-slice_fusion.5, f32[96,8,256]{2,1,0:T(8,128)} %get-tuple-element.235, bf16[1024,96,8]{0,2,1:T(8,128)(2,1)} %get-tuple-element.245, s32[]{:T(128)S(6)} %select_n.25, pred[]{:T(512)S(6)} %compare.7), kind=kOutput, calls=%fused_computation.16.clone.3 | convolution fusion | flops 214302720 | bytes 2555909 | tf_op jit(solution)/shard_map/while/body/eval_jaxpr/bms,bmk->msk/dot_general | solution.py:18
  265.0 12.2 %fusion.32 = f32[96,8,256]{2,1,0:T(8,128)} fusion(s32[512,96]{0,1:T(8,128)S(1)} %constant_dynamic-slice_fusion.5, f32[96,8,256]{2,1,0:T(8,128)} %get-tuple-element.235, bf16[1024,96,8]{0,2,1:T(8,128)(2,1)} %get-tuple-element.245, s32[]{:T(128)S(6)} %select_n.25, pred[]{:T(512)S(6)} %compare.7), kind=kOutput, calls=%fused_computation.16.clone.3 | convolution fusion | flops 214302720 | bytes 2555909 | tf_op jit(solution)/shard_map/while/body/eval_jaxpr/bms,bmk->msk/dot_general | solution.py:18
  279.2 55.9 %while.24 = (s32[]{:T(128)}, f32[3,8,256]{2,1,0:T(8,128)S(1)}, f32[3,256]{1,0:T(4,128)S(1)}, s32[4]{0:T(128)S(1)}, bf16[32768,3,8]{0,2,1:T(8,128)(2,1)}, /*index...) while((s32[]{:T(128)}, f32[3,8,256]{2,1,0:T(8,128)S(1)}, f32[3,256]{1,0:T(4,128)S(1)}, ...), condition=%wide.region_2.3_spmd.clone, body=%wide.region_0.2_spmd.clone.sunk | while | flops 132133640 | bytes 848030 | solution.py:25
  283.0 5.6 %fusion.30 = f32[3,8,256]{2,1,0:T(8,128)S(1)} fusion(s32[8192,3]{0,1:T(4,128)S(1)} %constant_dynamic-slice_fusion.4, bf16[32768,3,8]{0,2,1:T(8,128)(2,1)} %get-tuple-element.221, s32[]{:T(128)S(6)} %select_n.24, f32[3,8,256]{2,1,0:T(8,128)S(1)} %get-tuple-element.209, pred[]{:T(512)S(6)} %compare.6), kind=kOutput, calls=%fused_computation.8.clone.1 | convolution fusion | flops 106967040 | bytes 540677 | tf_op jit(solution)/shard_map/while/body/eval_jaxpr/bms,bmk->msk/dot_general | solution.py:18
  288.6 4.6 convert_reduce_fusion.2
  297.0 5.6 %fusion.30 = f32[3,8,256]{2,1,0:T(8,128)S(1)} fusion(s32[8192,3]{0,1:T(4,128)S(1)} %constant_dynamic-slice_fusion.4, bf16[32768,3,8]{0,2,1:T(8,128)(2,1)} %get-tuple-element.221, s32[]{:T(128)S(6)} %select_n.24, f32[3,8,256]{2,1,0:T(8,128)S(1)} %get-tuple-element.209, pred[]{:T(512)S(6)} %compare.6), kind=kOutput, calls=%fused_computation.8.clone.1 | convolution fusion | flops 106967040 | bytes 540677 | tf_op jit(solution)/shard_map/while/body/eval_jaxpr/bms,bmk->msk/dot_general | solution.py:18
  302.6 4.6 convert_reduce_fusion.2
  310.9 5.6 %fusion.30 = f32[3,8,256]{2,1,0:T(8,128)S(1)} fusion(s32[8192,3]{0,1:T(4,128)S(1)} %constant_dynamic-slice_fusion.4, bf16[32768,3,8]{0,2,1:T(8,128)(2,1)} %get-tuple-element.221, s32[]{:T(128)S(6)} %select_n.24, f32[3,8,256]{2,1,0:T(8,128)S(1)} %get-tuple-element.209, pred[]{:T(512)S(6)} %compare.6), kind=kOutput, calls=%fused_computation.8.clone.1 | convolution fusion | flops 106967040 | bytes 540677 | tf_op jit(solution)/shard_map/while/body/eval_jaxpr/bms,bmk->msk/dot_general | solution.py:18
  316.5 4.6 convert_reduce_fusion.2
  324.9 5.6 %fusion.30 = f32[3,8,256]{2,1,0:T(8,128)S(1)} fusion(s32[8192,3]{0,1:T(4,128)S(1)} %constant_dynamic-slice_fusion.4, bf16[32768,3,8]{0,2,1:T(8,128)(2,1)} %get-tuple-element.221, s32[]{:T(128)S(6)} %select_n.24, f32[3,8,256]{2,1,0:T(8,128)S(1)} %get-tuple-element.209, pred[]{:T(512)S(6)} %compare.6), kind=kOutput, calls=%fused_computation.8.clone.1 | convolution fusion | flops 106967040 | bytes 540677 | tf_op jit(solution)/shard_map/while/body/eval_jaxpr/bms,bmk->msk/dot_general | solution.py:18
  335.1 143.1 %reduce-scatter.2.cloned.1.call-done = bf16[3,8,256]{2,1,0:T(8,128)(2,1)} async-done(((bf16[96,8,256]{2,1,0:T(8,128)(2,1)}), bf16[3,8,256]{2,1,0:T(8,128)(2,1)}) %reduce-scatter.2.cloned.1.call-update) | async-done | bytes 12304 | tf_op jit(solution)/shard_map/reduce_scatter | solution.py:79
  478.9 26.2 %all-reduce = (f32[3,8,256]{2,1,0:T(8,128)S(1)}, f32[3,256]{1,0:T(4,128)S(1)}) all-reduce(f32[3,8,256]{2,1,0:T(8,128)S(1)} %convert_subtract_fusion, f32[3,256]{1,0:T(4,128)S(1)} %get-tuple-element.67), channel_id=1, replica_groups=mesh['rows'=32,'tab'=8] {'tab'}, use_global_device_ids=true, to_apply=%region_10.11 | all-reduce | flops 6912 | bytes 55296 | tf_op jit(solution)/shard_map/psum | solution.py:82
  (66 shorter events, 54.7 us)
Async XLA Ops:
  6.5 42.8 %copy-start = (bf16[2048,768]{1,0:T(8,128)(2,1)S(1)}, bf16[2048,768]{1,0:T(8,128)(2,1)}, u32[]{:S(2)}) copy-start(bf16[2048,768]{1,0:T(8,128)(2,1)} %param.15) | copy-start | bytes 9437188
  7.7 1.0 copy-start.1
  10.0 0.7 copy-start.2
  58.8 75.9 %all-to-all-start.4 = ((bf16[32,8,8,768]{3,2,1,0:T(8,128)(2,1)}), bf16[32,8,8,768]{3,2,1,0:T(8,128)(2,1)}, u32[]{:S(2)}, u32[]{:S(2)}) async-start(bf16[32,8,8,768]{3,2,1,0:T(8,128)(2,1)} %bitcast.45), calls=%async_computation.4 | async-start | bytes 6291456 | tf_op jit(solution)/shard_map/all_to_all | solution.py:56
  134.7 45.3 %all-to-all-start = ((bf16[1024,32,24]{0,2,1:T(8,128)(2,1)}), bf16[1024,32,24]{0,2,1:T(8,128)(2,1)}, u32[]{:S(2)}, u32[]{:S(2)}) async-start(bf16[1024,32,24]{0,2,1:T(8,128)(2,1)} %bitcast.46), calls=%async_computation | async-start | bytes 3145728 | tf_op jit(solution)/shard_map/all_to_all | solution.py:72
  180.0 44.1 %all-to-all-start.5 = ((bf16[32,8,8,768]{3,2,0,1:T(8,128)(2,1)}), bf16[32,8,8,768]{3,2,0,1:T(8,128)(2,1)}, u32[]{:S(2)}, u32[]{:S(2)}) async-start(bf16[32,8,8,768]{3,2,0,1:T(8,128)(2,1)} %copy.26), calls=%async_computation.5 | async-start | bytes 6291456 | tf_op jit(solution)/shard_map/all_to_all | solution.py:55
  224.1 55.0 %all-to-all-start.1 = ((s32[1024,32,3]{0,2,1:T(4,128)}), s32[1024,32,3]{0,2,1:T(4,128)}, u32[]{:S(2)}, u32[]{:S(2)}) async-start(s32[1024,32,3]{0,2,1:T(4,128)} %reshape.54), calls=%async_computation.1 | async-start | bytes 1048576 | tf_op jit(solution)/shard_map/all_to_all | solution.py:73
  229.8 248.4 %reduce-scatter.2.cloned.1.call-start = ((), (), s32[]{:S(2)}) async-start(), calls=%async_computation.7 | async-start | bytes 405504 | tf_op jit(solution)/shard_map/reduce_scatter | solution.py:79
  279.2 225.9 %copy-start.3 = (f32[3,8,256]{2,1,0:T(8,128)S(1)}, f32[3,8,256]{2,1,0:T(8,128)}, u32[]{:S(2)}) copy-start(f32[3,8,256]{2,1,0:T(8,128)} %param.17) | copy-start | bytes 73732
Sparse Core Ops, SparseCore 0:
  279.3 198.8 reduce-scatter.1
where the time goes:
time: 515 us; the launch traced here: 513 us
  waiting for transfers between devices  272 us (53%)
  blocking collectives  58.1 us (11%)
  matrix products  55.4 us (11%)
  local copies, waits for them, and re-layouts  52.5 us (10%)
  starting transfers between devices  24.7 us (5%)
  other arithmetic  24.2 us (5%)
  between operations  13.6 us (3%)
  loops' own time  11.9 us (2%)
    reduce_scatter x1, waiting for transfers between devices, body(): lax.psum_scatter(centre_sums.astype(jnp.bfloat16), 'rows', scatter_dimens...  143 us
    all_to_all x1, waiting for transfers between devices, body(): lax.all_to_all(answers, 'rows', split_axis=0, concat_axis=0, tiled=True)  66.7 us
    dot_general x6, matrix products, accumulate(): jnp.einsum('bms,bmk->msk', pieces, one_hot, preferred_element_type=jnp.fl...  46.7 us
    all_to_all x1, waiting for transfers between devices, body(): lax.all_to_all(data_parts, 'rows', split_axis=1, concat_axis=0, tiled=True)  34 us
    all_to_all x1, waiting for transfers between devices, body(): lax.all_to_all(lax.all_to_all(answers, 'rows', split_axis=0, concat_axis=...  28.4 us
    psum x1, blocking collectives, body(): word_sums, word_counts = lax.psum((word_sums, word_counts), 'tab')  26.2 us
    all_to_all x1, blocking collectives, body(): lax.all_to_all(wanted, 'rows', split_axis=0, concat_axis=0, tiled=True)  21.2 us
    reduce_sum x4, other arithmetic, accumulate(): tallies = jnp.sum(one_hot, axis=0, dtype=jnp.float32)  18.2 us
  transfers between devices with their start and end apart: 5, of which 4 were waited for; matrix products, arithmetic and copies ran while one was open for 22% of the time, Pallas kernels for 0%

commit v1 on v0

v1 whole, which is shorter than its diff:
```python
import functools

import jax
import jax.numpy as jnp
from jax import lax
from jax.experimental import pallas as pl
from jax.experimental.pallas import tpu as pltpu
from jax.sharding import PartitionSpec as P

FIELDS = 128
LOW = 32
BF16 = jnp.bfloat16
F32 = jnp.float32
I32 = jnp.int32
NT = (((1,), (1,)), ((), ()))


def iota(shape, axis):
    return lax.broadcasted_iota(I32, shape, axis)


def route_kernel(devices, owner_ref, slot_ref, codes_ref, message_ref):
    subspaces, rows = codes_ref.shape
    places = message_ref.shape[0]
    cap = places // devices
    owner = owner_ref[...]
    same = iota((devices, rows), 0) == owner
    before = (iota((rows, rows), 0) < iota((rows, rows), 1)).astype(F32).astype(BF16)
    rank = jnp.dot(same.astype(F32).astype(BF16), before, preferred_element_type=F32)
    rank = jnp.sum(jnp.where(same, rank, 0.0), axis=0, keepdims=True)
    place = owner * cap + rank.astype(I32)
    slot = slot_ref[...]
    line = iota((FIELDS - subspaces, rows), 0)
    extra = jnp.where(line == 0, slot >> 4, jnp.where(line == 1, slot & 15, (line == 2).astype(I32)))
    info = jnp.concatenate([codes_ref[...], extra], axis=0).astype(F32).astype(BF16)
    step = 256
    for start in range(0, places, step):
        hit = ((iota((step, rows), 0) + start) == place).astype(F32).astype(BF16)
        message_ref[start : start + step, :] = lax.dot_general(
            hit, info, NT, preferred_element_type=F32
        ).astype(BF16)


def sums_kernel(
    vectors_ref, codes_ref, requests_ref, centroids_ref, rotation_ref,
    sums_ref, counts_ref,
    parts, high, low, left, right, turned, flipped,
):
    subspaces, rows = codes_ref.shape
    lists, width = centroids_ref.shape
    asked = requests_ref.shape[0]
    total = rows + asked
    sub_width = width // subspaces
    codewords = sums_ref.shape[1]
    top = codewords // LOW

    unit = (iota((256, width), 0) == iota((256, width), 1)).astype(F32).astype(BF16)
    for start in range(0, width, 256):
        picker = ((iota((256, width), 0) + start) == iota((256, width), 1)).astype(F32).astype(BF16)
        flipped[start : start + 256, :] = lax.dot_general(
            picker, rotation_ref[...], NT, preferred_element_type=F32
        ).astype(BF16)
    for start in range(0, rows, 256):
        parts[:, start : start + 256] = lax.dot_general(
            flipped[...], vectors_ref[start : start + 256, :], NT, preferred_element_type=F32
        ).astype(BF16)
    for start in range(0, lists, 256):
        turned[:, start : start + 256] = lax.dot_general(
            flipped[...], centroids_ref[start : start + 256, :], NT, preferred_element_type=F32
        ).astype(BF16)

    codes = codes_ref[...]
    high[:, :rows] = (codes >> 5).astype(F32)
    low[:, :rows] = (codes & (LOW - 1)).astype(F32)
    step = 256
    small = unit[:FIELDS, :FIELDS]
    for start in range(0, asked, step):
        fields = lax.dot_general(
            small, requests_ref[start : start + step, :], NT, preferred_element_type=F32
        ).astype(I32)
        valid = fields[subspaces + 2 : subspaces + 3, :] > 0
        slot = fields[subspaces : subspaces + 1, :] * 16 + fields[subspaces + 1 : subspaces + 2, :]
        asked_codes = fields[:subspaces, :]
        here = slice(rows + start, rows + start + step)
        high[:, here] = jnp.where(valid, asked_codes >> 5, top + 1).astype(F32)
        low[:, here] = (asked_codes & (LOW - 1)).astype(F32)
        pick = (iota((lists, step), 0) == slot).astype(F32).astype(BF16)
        parts[:, here] = (-jnp.dot(turned[...], pick, preferred_element_type=F32)).astype(BF16)

    group = codewords // LOW
    lines = group * sub_width
    chunk = 512

    def one_group(index, carry):
        line = pl.multiple_of(index * group, group)
        wide = pl.multiple_of(index * lines, lines)
        for start in range(0, total, chunk):
            here = slice(start, start + chunk)
            high8 = high[pl.ds(line, group), here]
            low8 = low[pl.ds(line, group), here]
            piece = parts[pl.ds(wide, lines), here]
            spread = jnp.concatenate(
                [jnp.broadcast_to(high8[m : m + 1], (sub_width, chunk)) for m in range(group)], axis=0
            ).astype(BF16)
            for value in range(top):
                left[value * lines : (value + 1) * lines, here] = jnp.where(
                    spread == jnp.array(value, BF16), piece, jnp.zeros_like(piece)
                )
            row_id = iota((LOW, chunk), 0).astype(F32).astype(BF16)
            for m in range(group):
                row = jnp.broadcast_to(low8[m : m + 1], (LOW, chunk)).astype(BF16)
                right[m * LOW : (m + 1) * LOW, here] = jnp.where(
                    row == row_id, jnp.array(1, BF16), jnp.array(0, BF16)
                )
        crossed = lax.dot_general(left[...], right[...], NT, preferred_element_type=F32)
        high8 = high[pl.ds(line, group), :rows]
        marks = jnp.concatenate(
            [jnp.where(high8 == float(value), 1.0, 0.0) for value in range(top)], axis=0
        ).astype(BF16)
        tally = lax.dot_general(marks, right[:, :rows], NT, preferred_element_type=F32)

        def fold(crossing, count, per):
            owner = iota((count, codewords), 0) // per
            keep = owner == iota((count, codewords), 1) // LOW
            halves = [jnp.zeros((count, 128), F32) for _ in range(codewords // 128)]
            lane = iota((count, 128), 1) // LOW
            for value in range(top):
                block = jnp.where(keep, crossing[value * count : (value + 1) * count, :], 0.0)
                line_sum = block[:, :128] + block[:, 128:]
                line_sum = line_sum + pltpu.roll(line_sum, 64, 1)
                line_sum = line_sum + pltpu.roll(line_sum, 32, 1)
                at = value // 4
                halves[at] = halves[at] + jnp.where(lane == value % 4, line_sum, 0.0)
            return jnp.concatenate(halves, axis=1)

        sums_ref[pl.ds(wide, lines), :] = fold(crossed, lines, sub_width)
        counts_ref[pl.ds(line, group), :] = fold(tally, group, 1)
        return carry

    lax.fori_loop(0, subspaces // group, one_group, 0)


def in_vmem(count):
    return [pl.BlockSpec(memory_space=pltpu.VMEM)] * count


def route(owner, slot, codes_t, devices):
    rows = owner.shape[1]
    places = 2 * rows
    return pl.pallas_call(
        functools.partial(route_kernel, devices),
        out_shape=jax.ShapeDtypeStruct((places, FIELDS), BF16),
        in_specs=in_vmem(3),
        out_specs=pl.BlockSpec(memory_space=pltpu.VMEM),
    )(owner, slot, codes_t)


def local_sums(vectors, codes_t, requests, centroids, rotation, codewords):
    subspaces, rows = codes_t.shape
    lists, width = centroids.shape
    asked = requests.shape[0]
    total = rows + asked
    top = codewords // LOW
    return pl.pallas_call(
        sums_kernel,
        out_shape=[
            jax.ShapeDtypeStruct((width, codewords), F32),
            jax.ShapeDtypeStruct((subspaces, codewords), F32),
        ],
        in_specs=in_vmem(5),
        out_specs=in_vmem(2),
        scratch_shapes=[
            pltpu.VMEM((width, total), BF16),
            pltpu.VMEM((subspaces, total), F32),
            pltpu.VMEM((subspaces, total), F32),
            pltpu.VMEM((top * 64, total), BF16),
            pltpu.VMEM((codewords, total), BF16),
            pltpu.VMEM((width, lists), BF16),
            pltpu.VMEM((width, width), BF16),
        ],
    )(vectors, codes_t, requests, centroids, rotation)


def body(vectors, list_owner, list_slot, codes, centroids, rotation, old_codebooks):
    n_rows = lax.axis_size("rows")
    n_tab = lax.axis_size("tab")
    devices = n_rows * n_tab
    row_dev, width = vectors.shape
    own, sub_width, codewords = old_codebooks.shape
    cap = 2 * row_dev // devices
    codes_t = codes.T
    message = route(list_owner.reshape(1, row_dev), list_slot.reshape(1, row_dev), codes_t, devices)
    message = message.reshape(n_rows, n_tab, cap, FIELDS)
    message = lax.all_to_all(message, "rows", split_axis=0, concat_axis=0, tiled=True)
    message = lax.all_to_all(message, "tab", split_axis=1, concat_axis=1, tiled=True)
    requests = message.reshape(devices * cap, FIELDS)
    sums, counts = local_sums(vectors, codes_t, requests, centroids, rotation, codewords)
    coarse = jnp.floor(counts * (1 / 256)) * 256
    tallies = jnp.stack([coarse, counts - coarse], axis=1)
    share = jnp.concatenate(
        [sums.reshape(n_rows * own, sub_width, codewords), tallies], axis=1
    ).astype(BF16)
    share = share.reshape(n_rows, own * (sub_width + 2), codewords)
    share = lax.all_to_all(share, "rows", split_axis=0, concat_axis=0, tiled=True)
    share = jnp.sum(share.astype(F32), axis=0)
    share = lax.psum(share, "tab").reshape(own, sub_width + 2, codewords)
    word_sums = share[:, :sub_width]
    word_counts = share[:, sub_width] + share[:, sub_width + 1]
    prior = float(row_dev * devices // codewords)
    return (word_sums + prior * old_codebooks) / (word_counts[:, None, :] + prior)


def solution(mesh):
    return jax.shard_map(
        body,
        mesh=mesh,
        in_specs=(
            P(("rows", "tab"), None),
            P(("rows", "tab"), None),
            P(("rows", "tab")),
            P(("rows", "tab"), None),
            P(("rows", "tab"), None),
            P(),
            P("rows", None, None),
        ),
        out_specs=P("rows", None, None),
        check_vma=False,
    )
```

time: 515 us -> 129 us (0.25)
  waiting for transfers between devices: 272 us -> 0 us
  matrix products: 55.4 us -> 0 us
  local copies, waits for them, and re-layouts: 52.5 us -> 1.37 us
  Pallas kernels: 0 us -> 35.6 us
  blocking collectives: 58.1 us -> 87.8 us
  starting transfers between devices: 24.7 us -> 0 us
  other arithmetic: 24.2 us -> 3.13 us
  between operations: 13.6 us -> 0.08 us
  loops' own time: 11.9 us -> 0 us
    reduce_scatter x1 -> x0, waiting for transfers between devices: 143 us -> none  [body(): lax.psum_scatter(centre_sums.astype(jnp.bfloat16), 'rows', scatter_dimens...]
    all_to_all x4 -> x0, waiting for transfers between devices: 129 us -> none  [the longest x1 66.7 us: body(): lax.all_to_all(answers, 'rows', split_axis=0, concat_axis=0, tiled=True)]
    dot_general x8 -> x0, matrix products: 55.4 us -> none  [the longest x6 46.7 us: accumulate(): jnp.einsum('bms,bmk->msk', pieces, one_hot, preferred_element_type=jnp.fl...]
    pallas_call x0 -> x2, Pallas kernels: none -> 35.6 us  [the longest x1 31.9 us: local_sums(): pl.pallas_call(sums_kernel, out_shape=[jax.ShapeDtypeStruct((width, codew...]
    all_to_all x2 -> x3, blocking collectives: 31.9 us -> 63.6 us  [the longest x1 28.3 us: body(): lax.all_to_all(message, 'rows', split_axis=0, concat_axis=0, tiled=True)]
    all_to_all x4 -> x0, starting transfers between devices: 24.5 us -> none  [the longest x1 7.51 us: body(): lax.all_to_all(data_parts, 'rows', split_axis=1, concat_axis=0, tiled=True)]
    reduce_sum x5 -> x1, other arithmetic: 18.6 us -> 0.09 us  [body(): share = jnp.sum(share.astype(F32), axis=0)]
    gather x2 -> x0, local copies, waits for them, and re-layouts: 17.3 us -> none  [the longest x1 9.44 us: body(): answers = centroids[incoming]]
  transfers between devices with their start and end apart: 5 -> 0, of which waited for: 4 -> 0; matrix products, arithmetic and copies ran while one was open for 22% -> 0% of each run, Pallas kernels for 0% -> 0%
where the time goes in v1:
time: 129 us; the launch traced here: 128 us
  blocking collectives  87.8 us (68%)
  Pallas kernels  35.6 us (28%)
  other arithmetic  3.13 us (2%)
  local copies, waits for them, and re-layouts  1.37 us (1%)
    pallas_call x1, Pallas kernels, local_sums(): pl.pallas_call(sums_kernel, out_shape=[jax.ShapeDtypeStruct((width, codew...  31.9 us
    all_to_all x1, blocking collectives, body(): lax.all_to_all(message, 'rows', split_axis=0, concat_axis=0, tiled=True)  28.3 us
    psum x1, blocking collectives, body(): share = lax.psum(share, 'tab').reshape(own, sub_width + 2, codewords)  24.1 us
    all_to_all x1, blocking collectives, body(): lax.all_to_all(share, 'rows', split_axis=0, concat_axis=0, tiled=True)  19.5 us
    all_to_all x1, blocking collectives, body(): lax.all_to_all(message, 'tab', split_axis=1, concat_axis=1, tiled=True)  15.8 us
    pallas_call x1, Pallas kernels, route(): pl.pallas_call(functools.partial(route_kernel, devices), out_shape=jax.Sh...  3.77 us

profile of v1, /device:TPU:1, one launch (start us, length us, event | category | flops | bytes accessed | tf_op | source)
XLA Modules:
  0.0 128.0 jit_solution(12563768593603554028)
XLA Ops:
  0.0 3.8 %shard_map.73 = bf16[2048,128]{1,0:T(8,128)(2,1)} custom-call(s32[1,1024]{1,0:T(1,128)} %bitcast.19, s32[1,1024]{1,0:T(1,128)} %bitcast.20, s32[96,1024]{1,0:T(8,128)} %bitcast.16), custom_call_target="tpu_custom_call" | custom-call | tf_op jit(solution)/shard_map/pallas_call | solution.py:150
  3.8 28.3 %all_to_all.15 = bf16[32,8,8,128]{3,2,1,0:T(8,128)(2,1)S(1)} all-to-all(bf16[32,8,8,128]{3,2,1,0:T(8,128)(2,1)} %bitcast.14), channel_id=1, replica_groups=mesh['rows'=32,'tab'=8] {'rows'}, dimensions={0} | all-to-all | bytes 1048576 | tf_op jit(solution)/shard_map/all_to_all | solution.py:194
  32.1 0.1 copy.16
  32.2 15.8 %all_to_all.16 = bf16[32,8,8,128]{3,2,0,1:T(8,128)(2,1)S(1)} all-to-all(bf16[32,8,8,128]{3,2,0,1:T(8,128)(2,1)S(1)} %copy.16), channel_id=1, replica_groups=mesh['rows'=32,'tab'=8] {'tab'}, dimensions={1} | all-to-all | bytes 1048576 | tf_op jit(solution)/shard_map/all_to_all | solution.py:195
  48.0 0.9 copy.17
  49.0 31.9 %shard_map.74 = (f32[768,256]{1,0:T(8,128)}, f32[96,256]{1,0:T(8,128)}) custom-call(bf16[1024,768]{1,0:T(8,128)(2,1)} %vectors_ref.1, s32[96,1024]{1,0:T(8,128)} %bitcast.17, bf16[2048,128]{1,0:T(8,128)(2,1)} %bitcast.15, bf16[2048,768]{1,0:T(8,128)(2,1)} %centroids_ref.1, bf16[768,768]{1,0:T(8,128)(2,1)} %rotation_ref.1), custom_call_target="tpu_custom_call" | custom-call | tf_op jit(solution)/shard_map/pallas_call | solution.py:164
  80.8 1.2 convert_bitcast_fusion
  82.0 0.9 fusion.1
  82.9 0.1 copy.18
  83.0 0.1 copy.19
  83.1 0.3 pad_maximum_fusion
  83.4 0.0 copy-start
  83.4 0.2 convert_element_type.8
  83.6 19.5 %all_to_all.17 = bf16[32,30,256]{2,1,0:T(8,128)(2,1)S(1)} all-to-all(bf16[32,30,256]{2,1,0:T(8,128)(2,1)S(1)} %convert_element_type.8), channel_id=1, replica_groups=mesh['rows'=32,'tab'=8] {'rows'}, dimensions={0} | all-to-all | bytes 983040 | tf_op jit(solution)/shard_map/all_to_all | solution.py:204
  103.1 0.1 convert_reduce_fusion
  103.2 24.1 %psum.7 = f32[3,10,256]{2,1,0:T(8,128)S(1)} all-reduce(f32[3,10,256]{2,1,0:T(8,128)S(1)} %reshape.28), channel_id=1, replica_groups=mesh['rows'=32,'tab'=8] {'tab'}, use_global_device_ids=true, to_apply=%region_1.0 | all-reduce | flops 7680 | bytes 61440 | tf_op jit(solution)/shard_map/psum | solution.py:206
  127.4 0.0 copy-done
  127.4 0.6 fusion.3
  (3 shorter events, 0.0 us)
Async XLA Ops:
  83.4 44.0 %copy-start = (f32[3,8,256]{2,1,0:T(8,128)S(1)}, f32[3,8,256]{2,1,0:T(8,128)}, u32[]{:S(2)}) copy-start(f32[3,8,256]{2,1,0:T(8,128)} %param.13) | copy-start | bytes 73732

commit v2 on v1

--- a/solution.py
+++ b/solution.py
@@ -13,16 +13,29 @@
 F32 = jnp.float32
 I32 = jnp.int32
 NT = (((1,), (1,)), ((), ()))
+MESH = pl.DeviceIdType.MESH
 
 
 def iota(shape, axis):
     return lax.broadcasted_iota(I32, shape, axis)
 
 
-def route_kernel(devices, owner_ref, slot_ref, codes_ref, message_ref):
+def route_kernel(n_rows, n_tab, owner_ref, slot_ref, codes_ref, arrived_ref, message, arrived, sent_sem, got_sem):
+    devices = n_rows * n_tab
+    my_row, my_tab = lax.axis_index("rows"), lax.axis_index("tab")
+    me = my_row * n_tab + my_tab
+    barrier = pltpu.get_barrier_semaphore()
+
+    def greet(offset, carry):
+        peer = lax.rem(me + offset, devices)
+        pl.semaphore_signal(
+            barrier, inc=1, device_id=(peer // n_tab, lax.rem(peer, n_tab)), device_id_type=MESH
+        )
+        return carry
+
+    lax.fori_loop(1, devices, greet, 0)
     subspaces, rows = codes_ref.shape
-    places = message_ref.shape[0]
-    cap = places // devices
+    cap = message.shape[1]
     owner = owner_ref[...]
     same = iota((devices, rows), 0) == owner
     before = (iota((rows, rows), 0) < iota((rows, rows), 1)).astype(F32).astype(BF16)
@@ -33,18 +46,44 @@
     line = iota((FIELDS - subspaces, rows), 0)
     extra = jnp.where(line == 0, slot >> 4, jnp.where(line == 1, slot & 15, (line == 2).astype(I32)))
     info = jnp.concatenate([codes_ref[...], extra], axis=0).astype(F32).astype(BF16)
-    step = 256
-    for start in range(0, places, step):
+    step = min(256, devices * cap)
+    for start in range(0, devices * cap, step):
         hit = ((iota((step, rows), 0) + start) == place).astype(F32).astype(BF16)
-        message_ref[start : start + step, :] = lax.dot_general(
-            hit, info, NT, preferred_element_type=F32
-        ).astype(BF16)
+        piece = lax.dot_general(hit, info, NT, preferred_element_type=F32).astype(BF16)
+        message[start // cap : (start + step) // cap] = piece.reshape(step // cap, cap, FIELDS)
+    arrived[me] = message[me]
+    pl.semaphore_wait(barrier, devices - 1)
+
+    def send(offset, carry):
+        peer = lax.rem(me + offset, devices)
+        pltpu.make_async_remote_copy(
+            src_ref=message.at[peer],
+            dst_ref=arrived.at[me],
+            send_sem=sent_sem,
+            recv_sem=got_sem,
+            device_id=(peer // n_tab, lax.rem(peer, n_tab)),
+            device_id_type=MESH,
+        ).start()
+        return carry
+
+    lax.fori_loop(1, devices, send, 0)
+    everything = pltpu.make_async_remote_copy(
+        src_ref=message.at[pl.ds(0, devices - 1)],
+        dst_ref=arrived.at[pl.ds(0, devices - 1)],
+        send_sem=sent_sem,
+        recv_sem=got_sem,
+        device_id=(my_row, lax.rem(my_tab + 1, n_tab)),
+        device_id_type=MESH,
+    )
+    everything.wait_recv()
+    arrived_ref[...] = arrived[...].reshape(devices * cap, FIELDS)
+    everything.wait_send()
 
 
 def sums_kernel(
     vectors_ref, codes_ref, requests_ref, centroids_ref, rotation_ref,
-    sums_ref, counts_ref,
-    parts, high, low, left, right, turned, flipped,
+    pieces_ref,
+    sums_ref, counts_ref, parts, high, low, left, right, turned, flipped,
 ):
     subspaces, rows = codes_ref.shape
     lists, width = centroids_ref.shape
@@ -139,23 +178,158 @@
 
     lax.fori_loop(0, subspaces // group, one_group, 0)
 
+    n_rows = pieces_ref.shape[1]
+    own = subspaces // n_rows
+    counts = counts_ref[...]
+    coarse = jnp.floor(counts * (1 / 256)) * 256
+    fine = counts - coarse
+    gap = jnp.zeros((8 - 2 * own, 128), F32)
+    for r in range(n_rows):
+        mine = slice(r * own, (r + 1) * own)
+        for half in range(codewords // 128):
+            lanes = slice(half * 128, (half + 1) * 128)
+            for q in range(own):
+                at = (r * own + q) * sub_width
+                pieces_ref[2 * q + half, r] = sums_ref[at : at + sub_width, lanes].astype(BF16)
+            pieces_ref[2 * own + half, r] = jnp.concatenate(
+                [coarse[mine, lanes], fine[mine, lanes], gap], axis=0
+            ).astype(BF16)
+
+
+def collect_kernel(
+    n_rows, n_tab, prior, pieces_ref, old_ref, out_ref,
+    first, total, middle, second, mine, third,
+    sent1, got1, sent2, got2, sent3, got3,
+):
+    my_row, my_tab = lax.axis_index("rows"), lax.axis_index("tab")
+    barrier = pltpu.get_barrier_semaphore()
+
+    def row_peer(offset):
+        return lax.rem(my_row + offset, n_rows)
+
+    def tab_peer(offset):
+        return lax.rem(my_tab + offset, n_tab)
+
+    def greet_row(offset, carry):
+        pl.semaphore_signal(barrier, inc=1, device_id=(row_peer(offset), my_tab), device_id_type=MESH)
+        return carry
+
+    def greet_tab(offset, carry):
+        pl.semaphore_signal(barrier, inc=1, device_id=(my_row, tab_peer(offset)), device_id_type=MESH)
+        return carry
+
+    lax.fori_loop(1, n_tab, greet_tab, 0)
+    lax.fori_loop(1, n_rows, greet_row, 0)
+    pl.semaphore_wait(barrier, n_rows + n_tab - 2)
+
+    def copy1(source, slot, peer):
+        return pltpu.make_async_remote_copy(
+            src_ref=pieces_ref.at[source], dst_ref=first.at[slot],
+            send_sem=sent1.at[source], recv_sem=got1.at[slot],
+            device_id=(my_row, peer), device_id_type=MESH,
+        )
+
+    def start1(offset, carry):
+        copy1(tab_peer(offset), my_tab, tab_peer(offset)).start()
+        return carry
+
+    lax.fori_loop(1, n_tab, start1, 0)
+    total[...] = pieces_ref[my_tab].astype(F32)
+
+    def add1(offset, carry):
+        source = tab_peer(n_tab - offset)
+        copy1(tab_peer(offset), source, tab_peer(offset)).wait_recv()
+        total[...] += first[source].astype(F32)
+        return carry
+
+    lax.fori_loop(1, n_tab, add1, 0)
+    middle[...] = total[...].astype(BF16)
+
+    def copy2(source, slot, peer):
+        return pltpu.make_async_remote_copy(
+            src_ref=middle.at[source], dst_ref=second.at[slot],
+            send_sem=sent2.at[source], recv_sem=got2.at[slot],
+            device_id=(peer, my_tab), device_id_type=MESH,
+        )
+
+    def start2(offset, carry):
+        copy2(row_peer(offset), my_row, row_peer(offset)).start()
+        return carry
+
+    lax.fori_loop(1, n_rows, start2, 0)
+
+    def add2(offset, held):
+        source = row_peer(n_rows - offset)
+        copy2(row_peer(offset), source, row_peer(offset)).wait_recv()
+        return held + second[source].astype(F32)
+
+    mine[...] = lax.fori_loop(1, n_rows, add2, total[my_row])
+    third[my_tab] = mine[...]
+
+    def copy3(slot, peer):
+        return pltpu.make_async_remote_copy(
+            src_ref=mine, dst_ref=third.at[slot],
+            send_sem=sent3.at[peer], recv_sem=got3.at[slot],
+            device_id=(my_row, peer), device_id_type=MESH,
+        )
+
+    def start3(offset, carry):
+        copy3(my_tab, tab_peer(offset)).start()
+        return carry
+
+    lax.fori_loop(1, n_tab, start3, 0)
+
+    def wait3(offset, carry):
+        copy3(tab_peer(n_tab - offset), tab_peer(offset)).wait_recv()
+        return carry
+
+    lax.fori_loop(1, n_tab, wait3, 0)
+    own = out_ref.shape[0]
+    for half in range(out_ref.shape[2] // 128):
+        lanes = slice(half * 128, (half + 1) * 128)
+        counts = third[2 * own + half]
+        for q in range(own):
+            weight = counts[q : q + 1] + counts[own + q : own + q + 1] + prior
+            out_ref[q, :, lanes] = (third[2 * q + half] + prior * old_ref[q, :, lanes]) / weight
+
+    def drain_tab(offset, carry):
+        copy1(tab_peer(offset), my_tab, tab_peer(offset)).wait_send()
+        copy3(my_tab, tab_peer(offset)).wait_send()
+        return carry
+
+    def drain_row(offset, carry):
+        copy2(row_peer(offset), my_row, row_peer(offset)).wait_send()
+        return carry
+
+    lax.fori_loop(1, n_tab, drain_tab, 0)
+    lax.fori_loop(1, n_rows, drain_row, 0)
+
 
 def in_vmem(count):
     return [pl.BlockSpec(memory_space=pltpu.VMEM)] * count
 
 
-def route(owner, slot, codes_t, devices):
+def route(owner, slot, codes_t, n_rows, n_tab):
     rows = owner.shape[1]
+    devices = n_rows * n_tab
     places = 2 * rows
+    cap = places // devices
     return pl.pallas_call(
-        functools.partial(route_kernel, devices),
+        functools.partial(route_kernel, n_rows, n_tab),
         out_shape=jax.ShapeDtypeStruct((places, FIELDS), BF16),
         in_specs=in_vmem(3),
         out_specs=pl.BlockSpec(memory_space=pltpu.VMEM),
+        scratch_shapes=[
+            pltpu.VMEM((devices, cap, FIELDS), BF16),
+            pltpu.VMEM((devices, cap, FIELDS), BF16),
+            pltpu.SemaphoreType.DMA,
+            pltpu.SemaphoreType.DMA,
+        ],
+        compiler_params=pltpu.CompilerParams(collective_id=0, has_side_effects=True),
     )(owner, slot, codes_t)
 
 
-def local_sums(vectors, codes_t, requests, centroids, rotation, codewords):
+def local_sums(vectors, codes_t, requests, centroids, rotation, codewords, n_rows):
     subspaces, rows = codes_t.shape
     lists, width = centroids.shape
     asked = requests.shape[0]
@@ -163,13 +337,14 @@
     top = codewords // LOW
     return pl.pallas_call(
         sums_kernel,
-        out_shape=[
-            jax.ShapeDtypeStruct((width, codewords), F32),
-            jax.ShapeDtypeStruct((subspaces, codewords), F32),
-        ],
+        out_shape=jax.ShapeDtypeStruct(
+            ((subspaces // n_rows + 1) * (codewords // 128), n_rows, 8, 128), BF16
+        ),
         in_specs=in_vmem(5),
-        out_specs=in_vmem(2),
+        out_specs=pl.BlockSpec(memory_space=pltpu.VMEM),
         scratch_shapes=[
+            pltpu.VMEM((width, codewords), F32),
+            pltpu.VMEM((subspaces, codewords), F32),
             pltpu.VMEM((width, total), BF16),
             pltpu.VMEM((subspaces, total), F32),
             pltpu.VMEM((subspaces, total), F32),
@@ -181,33 +356,44 @@
     )(vectors, codes_t, requests, centroids, rotation)
 
 
+def collect(pieces, old_codebooks, prior, n_rows, n_tab):
+    piece = pieces.shape[2:]
+    return pl.pallas_call(
+        functools.partial(collect_kernel, n_rows, n_tab, prior),
+        out_shape=jax.ShapeDtypeStruct(old_codebooks.shape, F32),
+        in_specs=in_vmem(2),
+        out_specs=pl.BlockSpec(memory_space=pltpu.VMEM),
+        scratch_shapes=[
+            pltpu.VMEM((n_tab, n_rows, *piece), BF16),
+            pltpu.VMEM((n_rows, *piece), F32),
+            pltpu.VMEM((n_rows, *piece), BF16),
+            pltpu.VMEM((n_rows, *piece), BF16),
+            pltpu.VMEM(piece, F32),
+            pltpu.VMEM((n_tab, *piece), F32),
+            pltpu.SemaphoreType.DMA((n_tab,)),
+            pltpu.SemaphoreType.DMA((n_tab,)),
+            pltpu.SemaphoreType.DMA((n_rows,)),
+            pltpu.SemaphoreType.DMA((n_rows,)),
+            pltpu.SemaphoreType.DMA((n_tab,)),
+            pltpu.SemaphoreType.DMA((n_tab,)),
+        ],
+        compiler_params=pltpu.CompilerParams(collective_id=1, has_side_effects=True),
+    )(pieces, old_codebooks)
+
+
 def body(vectors, list_owner, list_slot, codes, centroids, rotation, old_codebooks):
     n_rows = lax.axis_size("rows")
     n_tab = lax.axis_size("tab")
     devices = n_rows * n_tab
     row_dev, width = vectors.shape
-    own, sub_width, codewords = old_codebooks.shape
-    cap = 2 * row_dev // devices
+    codewords = old_codebooks.shape[2]
     codes_t = codes.T
-    message = route(list_owner.reshape(1, row_dev), list_slot.reshape(1, row_dev), codes_t, devices)
-    message = message.reshape(n_rows, n_tab, cap, FIELDS)
-    message = lax.all_to_all(message, "rows", split_axis=0, concat_axis=0, tiled=True)
-    message = lax.all_to_all(message, "tab", split_axis=1, concat_axis=1, tiled=True)
-    requests = message.reshape(devices * cap, FIELDS)
-    sums, counts = local_sums(vectors, codes_t, requests, centroids, rotation, codewords)
-    coarse = jnp.floor(counts * (1 / 256)) * 256
-    tallies = jnp.stack([coarse, counts - coarse], axis=1)
-    share = jnp.concatenate(
-        [sums.reshape(n_rows * own, sub_width, codewords), tallies], axis=1
-    ).astype(BF16)
-    share = share.reshape(n_rows, own * (sub_width + 2), codewords)
-    share = lax.all_to_all(share, "rows", split_axis=0, concat_axis=0, tiled=True)
-    share = jnp.sum(share.astype(F32), axis=0)
-    share = lax.psum(share, "tab").reshape(own, sub_width + 2, codewords)
-    word_sums = share[:, :sub_width]
-    word_counts = share[:, sub_width] + share[:, sub_width + 1]
+    requests = route(
+        list_owner.reshape(1, row_dev), list_slot.reshape(1, row_dev), codes_t, n_rows, n_tab
+    )
+    pieces = local_sums(vectors, codes_t, requests, centroids, rotation, codewords, n_rows)
     prior = float(row_dev * devices // codewords)
-    return (word_sums + prior * old_codebooks) / (word_counts[:, None, :] + prior)
+    return collect(pieces, old_codebooks, prior, n_rows, n_tab)
 
 
 def solution(mesh):

time: 129 us -> 91.7 us (0.71)
  blocking collectives: 87.8 us -> 0 us
  Pallas kernels: 35.6 us -> 90.1 us
  other arithmetic: 3.13 us -> 0 us
    all_to_all x3 -> x0, blocking collectives: 63.6 us -> none  [the longest x1 28.3 us: body(): lax.all_to_all(message, 'rows', split_axis=0, concat_axis=0, tiled=True)]
    pallas_call x2 -> x3, Pallas kernels: 35.6 us -> 90.1 us  [the longest x1 31.9 us: local_sums(): pl.pallas_call(sums_kernel, out_shape=jax.ShapeDtypeStruct(((subspaces //...]
    psum x1 -> x0, blocking collectives: 24.1 us -> none  [body(): share = lax.psum(share, 'tab').reshape(own, sub_width + 2, codewords)]
    unnamed x3 -> x1, local copies, waits for them, and re-layouts: 0.01 us -> 1.35 us
where the time goes in v2:
time: 91.7 us; the launch traced here: 91.5 us
  Pallas kernels  90.1 us (98%)
  local copies, waits for them, and re-layouts  1.35 us (1%)
    pallas_call x1, Pallas kernels, local_sums(): pl.pallas_call(sums_kernel, out_shape=jax.ShapeDtypeStruct(((subspaces //...  31.9 us
    pallas_call x1, Pallas kernels, route(): pl.pallas_call(functools.partial(route_kernel, n_rows, n_tab), out_shape=...  31.5 us
    pallas_call x1, Pallas kernels, collect(): pl.pallas_call(functools.partial(collect_kernel, n_rows, n_tab, prior), o...  26.8 us

profile of v2, /device:TPU:1, one launch (start us, length us, event | category | flops | bytes accessed | tf_op | source)
XLA Modules:
  0.0 91.5 jit_solution(14099620294534706425)
XLA Ops:
  0.0 31.5 %shard_map.73.requests_ref = bf16[2048,128]{1,0:T(8,128)(2,1)} custom-call(s32[1,1024]{1,0:T(1,128)} %bitcast.5, s32[1,1024]{1,0:T(1,128)} %bitcast.6, s32[96,1024]{1,0:T(8,128)} %bitcast.3), custom_call_target="tpu_custom_call" | custom-call | tf_op jit(solution)/shard_map/pallas_call | solution.py:317
  31.5 31.9 %shard_map.74.pieces_ref = bf16[8,32,8,128]{3,2,1,0:T(8,128)(2,1)} custom-call(bf16[1024,768]{1,0:T(8,128)(2,1)} %vectors_ref.1, s32[96,1024]{1,0:T(8,128)} %bitcast.4, bf16[2048,128]{1,0:T(8,128)(2,1)} %shard_map.73.requests_ref, bf16[2048,768]{1,0:T(8,128)(2,1)} %centroids_ref.1, bf16[768,768]{1,0:T(8,128)(2,1)} %rotation_ref.1), custom_call_target="tpu_custom_call" | custom-call | tf_op jit(solution)/shard_map/pallas_call | solution.py:338
  63.4 26.8 %shard_map.75 = f32[3,8,256]{2,1,0:T(8,128)} custom-call(bf16[8,32,8,128]{3,2,1,0:T(8,128)(2,1)} %shard_map.74.pieces_ref, f32[3,8,256]{2,1,0:T(8,128)} %old_ref.1), custom_call_target="tpu_custom_call" | custom-call | tf_op jit(solution)/shard_map/pallas_call | solution.py:361
  90.2 1.3 %copy.9 = f32[3,8,256]{2,1,0:T(8,128)} copy(f32[3,8,256]{2,1,0:T(8,128)} %shard_map.75) | data formatting | bytes 49152

commit v3 on v2

v3 whole, which is shorter than its diff:
```python
import functools

import jax
import jax.numpy as jnp
from jax import lax
from jax.experimental import pallas as pl
from jax.experimental.pallas import tpu as pltpu
from jax.sharding import PartitionSpec as P

FIELDS = 128
LOW = 32
BF16 = jnp.bfloat16
F32 = jnp.float32
I32 = jnp.int32
NT = (((1,), (1,)), ((), ()))
MESH = pl.DeviceIdType.MESH


def iota(shape, axis):
    return lax.broadcasted_iota(I32, shape, axis)


def fused_kernel(
    n_rows, n_tab,
    owner_ref, slot_ref, codes_ref, vectors_hbm, centroids_hbm, rotation_hbm,
    out_ref,
    vectors_ref, centroids_ref, rotation_ref, load_sem,
    message, arrived, sent_sem, got_sem,
    sums, tallies, parts, high, low, left, right, turned, flipped,
    pieces, first, total, middle, second, mine, third,
    sent1, got1, sent2, got2, sent3, got3,
):
    devices = n_rows * n_tab
    my_row, my_tab = lax.axis_index("rows"), lax.axis_index("tab")
    me = my_row * n_tab + my_tab
    barrier = pltpu.get_barrier_semaphore()

    loads = [
        pltpu.make_async_copy(source, target, load_sem.at[number])
        for number, (source, target) in enumerate(
            [(rotation_hbm, rotation_ref), (vectors_hbm, vectors_ref), (centroids_hbm, centroids_ref)]
        )
    ]
    for load in loads:
        load.start()

    def greet(offset, carry):
        peer = lax.rem(me + offset, devices)
        pl.semaphore_signal(
            barrier, inc=1, device_id=(peer // n_tab, lax.rem(peer, n_tab)), device_id_type=MESH
        )
        return carry

    lax.fori_loop(1, devices, greet, 0)

    subspaces, rows = codes_ref.shape
    cap = message.shape[1]
    owner = owner_ref[...]
    same = iota((devices, rows), 0) == owner
    before = (iota((rows, rows), 0) < iota((rows, rows), 1)).astype(F32).astype(BF16)
    rank = jnp.dot(same.astype(F32).astype(BF16), before, preferred_element_type=F32)
    rank = jnp.sum(jnp.where(same, rank, 0.0), axis=0, keepdims=True)
    place = owner * cap + rank.astype(I32)
    slot = slot_ref[...]
    line = iota((FIELDS - subspaces, rows), 0)
    extra = jnp.where(line == 0, slot >> 4, jnp.where(line == 1, slot & 15, (line == 2).astype(I32)))
    info = jnp.concatenate([codes_ref[...], extra], axis=0).astype(F32).astype(BF16)
    step = min(256, devices * cap)
    for start in range(0, devices * cap, step):
        hit = ((iota((step, rows), 0) + start) == place).astype(F32).astype(BF16)
        piece = lax.dot_general(hit, info, NT, preferred_element_type=F32).astype(BF16)
        message[start // cap : (start + step) // cap] = piece.reshape(step // cap, cap, FIELDS)
    arrived[me] = message[me]
    pl.semaphore_wait(barrier, devices - 1)

    def send(offset, carry):
        peer = lax.rem(me + offset, devices)
        pltpu.make_async_remote_copy(
            src_ref=message.at[peer],
            dst_ref=arrived.at[me],
            send_sem=sent_sem,
            recv_sem=got_sem,
            device_id=(peer // n_tab, lax.rem(peer, n_tab)),
            device_id_type=MESH,
        ).start()
        return carry

    lax.fori_loop(1, devices, send, 0)

    lists, width = centroids_ref.shape
    asked = devices * cap
    sub_width = width // subspaces
    codewords = sums.shape[1]
    top = codewords // LOW
    group = codewords // LOW
    lines = group * sub_width

    codes = codes_ref[...]
    high[:, :rows] = (codes >> 5).astype(F32)
    low[:, :rows] = (codes & (LOW - 1)).astype(F32)
    loads[0].wait()
    for start in range(0, width, 256):
        picker = ((iota((256, width), 0) + start) == iota((256, width), 1)).astype(F32).astype(BF16)
        flipped[start : start + 256, :] = lax.dot_general(
            picker, rotation_ref[...], NT, preferred_element_type=F32
        ).astype(BF16)
    loads[1].wait()
    for start in range(0, rows, 256):
        parts[:, start : start + 256] = lax.dot_general(
            flipped[...], vectors_ref[start : start + 256, :], NT, preferred_element_type=F32
        ).astype(BF16)

    def fill(index, begin, end):
        line = pl.multiple_of(index * group, group)
        wide = pl.multiple_of(index * lines, lines)
        chunk = 512
        for start in range(begin, end, chunk):
            here = slice(start, start + chunk)
            high8 = high[pl.ds(line, group), here]
            low8 = low[pl.ds(line, group), here]
            piece = parts[pl.ds(wide, lines), here]
            spread = jnp.concatenate(
                [jnp.broadcast_to(high8[m : m + 1], (sub_width, chunk)) for m in range(group)], axis=0
            ).astype(BF16)
            for value in range(top):
                left[value * lines : (value + 1) * lines, here] = jnp.where(
                    spread == jnp.array(value, BF16), piece, jnp.zeros_like(piece)
                )
            row_id = iota((LOW, chunk), 0).astype(F32).astype(BF16)
            for m in range(group):
                row = jnp.broadcast_to(low8[m : m + 1], (LOW, chunk)).astype(BF16)
                right[m * LOW : (m + 1) * LOW, here] = jnp.where(
                    row == row_id, jnp.array(1, BF16), jnp.array(0, BF16)
                )
        return lax.dot_general(
            left[:, begin:end], right[:, begin:end], NT, preferred_element_type=F32
        )

    def fold(crossing, count, per):
        keep = iota((count, codewords), 0) // per == iota((count, codewords), 1) // LOW
        halves = [jnp.zeros((count, 128), F32) for _ in range(codewords // 128)]
        lane = iota((count, 128), 1) // LOW
        for value in range(top):
            block = jnp.where(keep, crossing[value * count : (value + 1) * count, :], 0.0)
            line_sum = block[:, :128] + block[:, 128:]
            line_sum = line_sum + pltpu.roll(line_sum, 64, 1)
            line_sum = line_sum + pltpu.roll(line_sum, 32, 1)
            at = value // 4
            halves[at] = halves[at] + jnp.where(lane == value % 4, line_sum, 0.0)
        return jnp.concatenate(halves, axis=1)

    def own_group(index, carry):
        line = pl.multiple_of(index * group, group)
        wide = pl.multiple_of(index * lines, lines)
        crossed = fill(index, 0, rows)
        high8 = high[pl.ds(line, group), :rows]
        marks = jnp.concatenate(
            [jnp.where(high8 == float(value), 1.0, 0.0) for value in range(top)], axis=0
        ).astype(BF16)
        tally = lax.dot_general(marks, right[:, :rows], NT, preferred_element_type=F32)
        sums[pl.ds(wide, lines), :] = fold(crossed, lines, sub_width)
        tallies[pl.ds(line, group), :] = fold(tally, group, 1)
        return carry

    lax.fori_loop(0, subspaces // group, own_group, 0)
    loads[2].wait()
    for start in range(0, lists, 256):
        turned[:, start : start + 256] = lax.dot_general(
            flipped[...], centroids_ref[start : start + 256, :], NT, preferred_element_type=F32
        ).astype(BF16)
    own = subspaces // n_rows
    counts = tallies[...]
    coarse = jnp.floor(counts * (1 / 256)) * 256
    fine = counts - coarse
    gap = jnp.zeros((8 - 2 * own, 128), F32)
    for r in range(n_rows):
        these = slice(r * own, (r + 1) * own)
        for half in range(codewords // 128):
            lanes = slice(half * 128, (half + 1) * 128)
            pieces[2 * own + half, r] = jnp.concatenate(
                [coarse[these, lanes], fine[these, lanes], gap], axis=0
            ).astype(BF16)

    everything = pltpu.make_async_remote_copy(
        src_ref=message.at[pl.ds(0, devices - 1)],
        dst_ref=arrived.at[pl.ds(0, devices - 1)],
        send_sem=sent_sem,
        recv_sem=got_sem,
        device_id=(my_row, lax.rem(my_tab + 1, n_tab)),
        device_id_type=MESH,
    )
    everything.wait_recv()
    small = (iota((FIELDS, FIELDS), 0) == iota((FIELDS, FIELDS), 1)).astype(F32).astype(BF16)
    for start in range(0, asked, step):
        wanted = arrived[start // cap : (start + step) // cap].reshape(step, FIELDS)
        fields = lax.dot_general(small, wanted, NT, preferred_element_type=F32).astype(I32)
        valid = fields[subspaces + 2 : subspaces + 3, :] > 0
        slot = fields[subspaces : subspaces + 1, :] * 16 + fields[subspaces + 1 : subspaces + 2, :]
        asked_codes = fields[:subspaces, :]
        here = slice(rows + start, rows + start + step)
        high[:, here] = jnp.where(valid, asked_codes >> 5, top + 1).astype(F32)
        low[:, here] = (asked_codes & (LOW - 1)).astype(F32)
        pick = (iota((lists, step), 0) == slot).astype(F32).astype(BF16)
        parts[:, here] = (-jnp.dot(turned[...], pick, preferred_element_type=F32)).astype(BF16)

    def tab_peer(offset):
        return lax.rem(my_tab + offset, n_tab)

    def row_peer(offset):
        return lax.rem(my_row + offset, n_rows)

    def asked_group(index, carry):
        wide = pl.multiple_of(index * lines, lines)
        folded = sums[pl.ds(wide, lines), :] + fold(fill(index, rows, rows + asked), lines, sub_width)
        for m in range(group):
            subspace = index * group + m
            r, q = subspace // own, lax.rem(subspace, own)
            for half in range(codewords // 128):
                pieces[2 * q + half, r] = folded[
                    m * sub_width : (m + 1) * sub_width, half * 128 : (half + 1) * 128
                ].astype(BF16)
        return carry

    lax.fori_loop(0, subspaces // group, asked_group, 0)

    def copy1(source, slot, peer):
        return pltpu.make_async_remote_copy(
            src_ref=pieces.at[source], dst_ref=first.at[slot],
            send_sem=sent1.at[source], recv_sem=got1.at[slot],
            device_id=(my_row, peer), device_id_type=MESH,
        )

    def start1(offset, carry):
        copy1(tab_peer(offset), my_tab, tab_peer(offset)).start()
        return carry

    lax.fori_loop(1, n_tab, start1, 0)
    total[...] = pieces[my_tab].astype(F32)

    def add1(offset, carry):
        source = tab_peer(n_tab - offset)
        copy1(tab_peer(offset), source, tab_peer(offset)).wait_recv()
        total[...] += first[source].astype(F32)
        return carry

    lax.fori_loop(1, n_tab, add1, 0)
    middle[...] = total[...].astype(BF16)

    def copy2(source, slot, peer):
        return pltpu.make_async_remote_copy(
            src_ref=middle.at[source], dst_ref=second.at[slot],
            send_sem=sent2.at[source], recv_sem=got2.at[slot],
            device_id=(peer, my_tab), device_id_type=MESH,
        )

    def start2(offset, carry):
        copy2(row_peer(offset), my_row, row_peer(offset)).start()
        return carry

    lax.fori_loop(1, n_rows, start2, 0)

    def add2(offset, held):
        source = row_peer(n_rows - offset)
        copy2(row_peer(offset), source, row_peer(offset)).wait_recv()
        return held + second[source].astype(F32)

    mine[...] = lax.fori_loop(1, n_rows, add2, total[my_row])
    third[my_tab] = mine[...]

    def copy3(slot, peer):
        return pltpu.make_async_remote_copy(
            src_ref=mine, dst_ref=third.at[slot],
            send_sem=sent3.at[peer], recv_sem=got3.at[slot],
            device_id=(my_row, peer), device_id_type=MESH,
        )

    def start3(offset, carry):
        copy3(my_tab, tab_peer(offset)).start()
        return carry

    lax.fori_loop(1, n_tab, start3, 0)
    everything.wait_send()

    def drain_tab(offset, carry):
        copy1(tab_peer(offset), my_tab, tab_peer(offset)).wait_send()
        return carry

    def drain_row(offset, carry):
        copy2(row_peer(offset), my_row, row_peer(offset)).wait_send()
        return carry

    def wait3(offset, carry):
        copy3(tab_peer(n_tab - offset), tab_peer(offset)).wait_recv()
        copy3(my_tab, tab_peer(offset)).wait_send()
        return carry

    lax.fori_loop(1, n_tab, drain_tab, 0)
    lax.fori_loop(1, n_rows, drain_row, 0)
    lax.fori_loop(1, n_tab, wait3, 0)
    for q in range(own + 1):
        for half in range(codewords // 128):
            out_ref[q, :, half * 128 : (half + 1) * 128] = third[2 * q + half]


def totals(owner, slot, codes_t, vectors, centroids, rotation, codewords, n_rows, n_tab):
    subspaces, rows = codes_t.shape
    lists, width = centroids.shape
    own = subspaces // n_rows
    devices = n_rows * n_tab
    asked = 2 * rows
    every = rows + asked
    top = codewords // LOW
    lines = top * (width // subspaces)
    vmem, anywhere = pl.BlockSpec(memory_space=pltpu.VMEM), pl.BlockSpec(memory_space=pl.ANY)
    dma = pltpu.SemaphoreType.DMA
    return pl.pallas_call(
        functools.partial(fused_kernel, n_rows, n_tab),
        out_shape=jax.ShapeDtypeStruct((own + 1, 8, codewords), F32),
        in_specs=[vmem] * 3 + [anywhere] * 3,
        out_specs=vmem,
        scratch_shapes=[
            pltpu.VMEM((rows, width), BF16),
            pltpu.VMEM((lists, width), BF16),
            pltpu.VMEM((width, width), BF16),
            dma((3,)),
            pltpu.VMEM((devices, asked // devices, FIELDS), BF16),
            pltpu.VMEM((devices, asked // devices, FIELDS), BF16),
            dma,
            dma,
            pltpu.VMEM((width, codewords), F32),
            pltpu.VMEM((subspaces, codewords), F32),
            pltpu.VMEM((width, every), BF16),
            pltpu.VMEM((subspaces, every), F32),
            pltpu.VMEM((subspaces, every), F32),
            pltpu.VMEM((top * lines, every), BF16),
            pltpu.VMEM((codewords, every), BF16),
            pltpu.VMEM((width, lists), BF16),
            pltpu.VMEM((width, width), BF16),
            pltpu.VMEM((n_tab, n_rows, 8, 128), BF16),
            pltpu.VMEM((n_tab, n_rows, 8, 128), BF16),
            pltpu.VMEM((n_rows, 8, 128), F32),
            pltpu.VMEM((n_rows, 8, 128), BF16),
            pltpu.VMEM((n_rows, 8, 128), BF16),
            pltpu.VMEM((8, 128), F32),
            pltpu.VMEM((n_tab, 8, 128), F32),
            dma((n_tab,)),
            dma((n_tab,)),
            dma((n_rows,)),
            dma((n_rows,)),
            dma((n_tab,)),
            dma((n_tab,)),
        ],
        compiler_params=pltpu.CompilerParams(collective_id=0, has_side_effects=True),
    )(owner, slot, codes_t, vectors, centroids, rotation)


def body(vectors, list_owner, list_slot, codes, centroids, rotation, old_codebooks):
    n_rows = lax.axis_size("rows")
    n_tab = lax.axis_size("tab")
    row_dev = vectors.shape[0]
    own, _, codewords = old_codebooks.shape
    summed = totals(
        list_owner.reshape(1, row_dev),
        list_slot.reshape(1, row_dev),
        codes.T,
        vectors,
        centroids,
        rotation,
        codewords,
        n_rows,
        n_tab,
    )
    prior = float(row_dev * n_rows * n_tab // codewords)
    counts = summed[own, :own] + summed[own, own : 2 * own]
    return (summed[:own] + prior * old_codebooks) / (counts[:, None, :] + prior)


def solution(mesh):
    return jax.shard_map(
        body,
        mesh=mesh,
        in_specs=(
            P(("rows", "tab"), None),
            P(("rows", "tab"), None),
            P(("rows", "tab")),
            P(("rows", "tab"), None),
            P(("rows", "tab"), None),
            P(),
            P("rows", None, None),
        ),
        out_specs=P("rows", None, None),
        check_vma=False,
    )
```

time: 91.7 us -> 74.1 us (0.81)
  Pallas kernels: 90.1 us -> 71.8 us
  other arithmetic: 0 us -> 2.13 us
  local copies, waits for them, and re-layouts: 1.35 us -> 0.01 us
    pallas_call x3 -> x1, Pallas kernels: 90.1 us -> 71.8 us  [totals(): pl.pallas_call(functools.partial(fused_kernel, n_rows, n_tab), out_shape=...]
    div x0 -> x1, other arithmetic: none -> 1.36 us  [body(): return (summed[:own] + prior * old_codebooks) / (counts[:, None, :] + prior)]
    unnamed x1 -> x2, local copies, waits for them, and re-layouts: 1.35 us -> 0.01 us
where the time goes in v3:
time: 74.1 us; the launch traced here: 73.9 us
  Pallas kernels  71.8 us (97%)
  other arithmetic  2.13 us (3%)
    pallas_call x1, Pallas kernels, totals(): pl.pallas_call(functools.partial(fused_kernel, n_rows, n_tab), out_shape=...  71.8 us

profile of v3, /device:TPU:1, one launch (start us, length us, event | category | flops | bytes accessed | tf_op | source)
XLA Modules:
  0.0 73.9 jit_solution(2979085057655049899)
XLA Ops:
  0.0 0.0 copy-start
  0.0 71.8 %shard_map.73 = f32[4,8,256]{2,1,0:T(8,128)} custom-call(s32[1,1024]{1,0:T(1,128)} %bitcast.6, s32[1,1024]{1,0:T(1,128)} %bitcast.7, s32[96,1024]{1,0:T(8,128)} %bitcast.5, bf16[1024,768]{1,0:T(8,128)(2,1)} %vectors_hbm.1, bf16[2048,768]{1,0:T(8,128)(2,1)} %centroids_hbm.1, bf16[768,768]{1,0:T(8,128)(2,1)} %rotation_hbm.1), custom_call_target="tpu_custom_call" | custom-call | tf_op jit(solution)/shard_map/pallas_call | solution.py:316
  71.8 0.8 %add_bitcast_fusion = f32[3,256]{1,0:T(4,128)S(1)} fusion(f32[4,8,256]{2,1,0:T(8,128)} %shard_map.73), kind=kLoop, calls=%fused_computation.1 | loop fusion | flops 1536 | bytes 9216 | tf_op jit(solution)/shard_map/add | solution.py:375
  72.6 0.0 copy-done
  72.6 1.4 %add_divide_fusion = f32[3,8,256]{2,1,0:T(8,128)} fusion(f32[3,8,256]{2,1,0:T(8,128)S(1)} %copy-done, f32[4,8,256]{2,1,0:T(8,128)} %shard_map.73, f32[3,256]{1,0:T(4,128)S(1)} %add_bitcast_fusion), kind=kLoop, calls=%fused_computation | loop fusion | flops 18432 | bytes 76800 | tf_op jit(solution)/shard_map/div | solution.py:375
Async XLA Ops:
  0.0 72.6 %copy-start = (f32[3,8,256]{2,1,0:T(8,128)S(1)}, f32[3,8,256]{2,1,0:T(8,128)}, u32[]{:S(2)}) copy-start(f32[3,8,256]{2,1,0:T(8,128)} %param.13) | copy-start | bytes 73732

commit v4 on v3

v4 whole, which is shorter than its diff:
```python
import functools

import jax
import jax.numpy as jnp
from jax import lax
from jax.experimental import pallas as pl
from jax.experimental.pallas import tpu as pltpu
from jax.sharding import PartitionSpec as P

FIELDS = 128
LOW = 32
UNITS = 3
PLANES = 8
BF16 = jnp.bfloat16
F32 = jnp.float32
I32 = jnp.int32
NT = (((1,), (1,)), ((), ()))
MESH = pl.DeviceIdType.MESH


def iota(shape, axis):
    return lax.broadcasted_iota(I32, shape, axis)


def fused_kernel(
    n_rows, n_tab, prior,
    owner_ref, slot_ref, codes_ref, old_ref, vectors_hbm, centroids_hbm, rotation_hbm,
    out_ref,
    vectors_ref, centroids_ref, rotation_ref, load_sem,
    message, arrived, sent_sem, got_sem,
    sums, tallies, parts, high, low, left, right, turned, flipped,
    pieces, first, total, middle, second, mine, third,
    sent1, got1, sent2, got2, sent3, got3,
):
    devices = n_rows * n_tab
    my_row, my_tab = lax.axis_index("rows"), lax.axis_index("tab")
    me = my_row * n_tab + my_tab
    barrier = pltpu.get_barrier_semaphore()

    loads = [
        pltpu.make_async_copy(source, target, load_sem.at[number])
        for number, (source, target) in enumerate(
            [(rotation_hbm, rotation_ref), (vectors_hbm, vectors_ref), (centroids_hbm, centroids_ref)]
        )
    ]
    for load in loads:
        load.start()

    def device(peer):
        return (peer // n_tab, lax.rem(peer, n_tab))

    def greet(offset, carry):
        pl.semaphore_signal(
            barrier, inc=1, device_id=device(lax.rem(me + offset, devices)), device_id_type=MESH
        )
        return carry

    lax.fori_loop(1, devices, greet, 0)

    subspaces, rows = codes_ref.shape
    cap = message.shape[1]
    owner = owner_ref[...]
    same = iota((devices, rows), 0) == owner
    before = (iota((rows, rows), 0) < iota((rows, rows), 1)).astype(F32).astype(BF16)
    rank = jnp.dot(same.astype(F32).astype(BF16), before, preferred_element_type=F32)
    rank = jnp.sum(jnp.where(same, rank, 0.0), axis=0, keepdims=True)
    place = owner * cap + rank.astype(I32)
    slot = slot_ref[...]
    line = iota((FIELDS - subspaces, rows), 0)
    extra = jnp.where(line == 0, slot >> 4, jnp.where(line == 1, slot & 15, (line == 2).astype(I32)))
    info = jnp.concatenate([codes_ref[...], extra], axis=0).astype(F32).astype(BF16)
    step = 256
    for start in range(0, devices * cap, step):
        hit = ((iota((step, rows), 0) + start) == place).astype(F32).astype(BF16)
        piece = lax.dot_general(hit, info, NT, preferred_element_type=F32).astype(BF16)
        message[start // cap : (start + step) // cap] = piece.reshape(step // cap, cap, FIELDS)

    plane = devices // PLANES
    block = 2 * plane
    my_plane, my_place = me // plane, lax.rem(me, plane)
    arrived[block - 1] = message[me]
    loads[0].wait()
    width = rotation_ref.shape[0]
    for start in range(0, width, 256):
        picker = ((iota((256, width), 0) + start) == iota((256, width), 1)).astype(F32).astype(BF16)
        flipped[start : start + 256, :] = lax.dot_general(
            picker, rotation_ref[...], NT, preferred_element_type=F32
        ).astype(BF16)
    pl.semaphore_wait(barrier, devices - 1)

    def ask(number, away, turn, at):
        peer = lax.rem(my_plane + away, PLANES) * plane + lax.rem(my_place + turn, plane)
        pltpu.make_async_remote_copy(
            src_ref=message.at[peer],
            dst_ref=arrived.at[number * block + at],
            send_sem=sent_sem,
            recv_sem=got_sem.at[number],
            device_id=device(peer),
            device_id_type=MESH,
        ).start()

    for number in range(PLANES // 2):

        def send(turn, carry, number=number):
            ask(number, PLANES // 2 - number, turn, turn)
            if number == 0:

                @pl.when(turn < plane - 1)
                def _():
                    ask(0, 0, turn + 1, plane + turn)
            else:
                ask(number, PLANES // 2 + number, turn, plane + turn)
            return carry

        lax.fori_loop(0, plane, send, 0)

    lists = centroids_ref.shape[0]
    asked = devices * cap
    sub_width = width // subspaces
    codewords = sums.shape[1]
    top = codewords // LOW
    group = codewords // LOW
    lines = group * sub_width
    own = subspaces // n_rows

    codes = codes_ref[...]
    high[:, :rows] = (codes >> 5).astype(F32)
    low[:, :rows] = (codes & (LOW - 1)).astype(F32)
    loads[1].wait()
    for start in range(0, rows, 256):
        parts[:, start : start + 256] = lax.dot_general(
            flipped[...], vectors_ref[start : start + 256, :], NT, preferred_element_type=F32
        ).astype(BF16)

    def fill(index, unit, begin, end, counted):
        line = pl.multiple_of(index * group, group)
        wide = pl.multiple_of(index * lines, lines)
        chunk = 512
        for start in range(begin, end, chunk):
            here = slice(start, start + chunk)
            there = slice(start - begin, start - begin + chunk)
            high8 = high[pl.ds(line, group), here]
            low8 = low[pl.ds(line, group), here]
            piece = parts[pl.ds(wide, lines), here]
            spread = jnp.concatenate(
                [jnp.broadcast_to(high8[m : m + 1], (sub_width, chunk)) for m in range(group)], axis=0
            ).astype(BF16)
            for value in range(top):
                left[unit, value * lines : (value + 1) * lines, there] = jnp.where(
                    spread == jnp.array(value, BF16), piece, jnp.zeros_like(piece)
                )
            if counted:
                left[unit, top * lines : top * (lines + group), there] = jnp.concatenate(
                    [jnp.where(high8 == float(value), 1.0, 0.0) for value in range(top)], axis=0
                ).astype(BF16)
            row_id = iota((LOW, chunk), 0).astype(F32).astype(BF16)
            for m in range(group):
                row = jnp.broadcast_to(low8[m : m + 1], (LOW, chunk)).astype(BF16)
                right[unit, m * LOW : (m + 1) * LOW, there] = jnp.where(
                    row == row_id, jnp.array(1, BF16), jnp.array(0, BF16)
                )

    def product(unit, depth, count):
        return lax.dot_general(
            left[unit, :count, :depth], right[unit, :, :depth], NT, preferred_element_type=F32
        )

    def fold(crossing, count, per):
        subspace = iota((count, 128), 0) // per
        quarter, lane = subspace & 3, iota((count, 128), 1) // LOW
        halves = []
        for half in range(codewords // 128):
            picked = [
                jnp.where(
                    subspace < 4,
                    crossing[value * count : (value + 1) * count, :128],
                    crossing[value * count : (value + 1) * count, 128:],
                )
                for value in range(4 * half, 4 * half + 4)
            ]
            moved = jnp.zeros((count, 128), F32)
            for turn in range(4):
                mixed = picked[0]
                for value in range(4):
                    mixed = jnp.where(lane == ((value - turn) & 3), picked[value], mixed)
                if turn:
                    mixed = pltpu.roll(mixed, LOW * turn, 1)
                moved = jnp.where(((lane - quarter) & 3) == turn, mixed, moved)
            halves.append(moved)
        return jnp.concatenate(halves, axis=1)

    def own_groups(index, carry):
        for unit in range(UNITS):
            fill(index * UNITS + unit, unit, 0, rows, True)
        for unit in range(UNITS):
            line = pl.multiple_of((index * UNITS + unit) * group, group)
            wide = pl.multiple_of((index * UNITS + unit) * lines, lines)
            crossed = product(unit, rows, top * (lines + group))
            sums[pl.ds(wide, lines), :] = fold(crossed[: top * lines], lines, sub_width)
            tallies[pl.ds(line, group), :] = fold(crossed[top * lines :], group, 1)
        return carry

    steps = subspaces // (group * UNITS)
    lax.fori_loop(0, steps, own_groups, 0)
    loads[2].wait()
    for start in range(0, lists, 256):
        turned[:, start : start + 256] = lax.dot_general(
            flipped[...], centroids_ref[start : start + 256, :], NT, preferred_element_type=F32
        ).astype(BF16)
    counts = tallies[...]
    coarse = jnp.floor(counts * (1 / 256)) * 256
    fine = counts - coarse
    gap = jnp.zeros((8 - 2 * own, 128), F32)
    for r in range(n_rows):
        these = slice(r * own, (r + 1) * own)
        for half in range(codewords // 128):
            lanes = slice(half * 128, (half + 1) * 128)
            pieces[2 * own + half, r] = jnp.concatenate(
                [coarse[these, lanes], fine[these, lanes], gap], axis=0
            ).astype(BF16)

    small = (iota((FIELDS, FIELDS), 0) == iota((FIELDS, FIELDS), 1)).astype(F32).astype(BF16)
    next_door = (my_row, lax.rem(my_tab + 1, n_tab))
    for number in range(PLANES // 2):
        count = block - 1 if number == 0 else block
        pltpu.make_async_remote_copy(
            src_ref=message.at[pl.ds(0, count)],
            dst_ref=arrived.at[pl.ds(number * block, count)],
            send_sem=sent_sem,
            recv_sem=got_sem.at[number],
            device_id=next_door,
            device_id_type=MESH,
        ).wait_recv()
        for start in range(number * block * cap, (number + 1) * block * cap, step):
            wanted = arrived[start // cap : (start + step) // cap].reshape(step, FIELDS)
            fields = lax.dot_general(small, wanted, NT, preferred_element_type=F32).astype(I32)
            valid = fields[subspaces + 2 : subspaces + 3, :] > 0
            slot = fields[subspaces : subspaces + 1, :] * 16 + fields[subspaces + 1 : subspaces + 2, :]
            asked_codes = fields[:subspaces, :]
            here = slice(rows + start, rows + start + step)
            high[:, here] = jnp.where(valid, asked_codes >> 5, top + 1).astype(F32)
            low[:, here] = (asked_codes & (LOW - 1)).astype(F32)
            pick = (iota((lists, step), 0) == slot).astype(F32).astype(BF16)
            parts[:, here] = (-jnp.dot(turned[...], pick, preferred_element_type=F32)).astype(BF16)

    def tab_peer(offset):
        return lax.rem(my_tab + offset, n_tab)

    def row_peer(offset):
        return lax.rem(my_row + offset, n_rows)

    share = n_rows // steps

    def copy1(index, source, slot, peer):
        rows_here = pl.ds(index * share, share)
        return pltpu.make_async_remote_copy(
            src_ref=pieces.at[source, rows_here], dst_ref=first.at[slot, rows_here],
            send_sem=sent1.at[index, source], recv_sem=got1.at[index, slot],
            device_id=(my_row, peer), device_id_type=MESH,
        )

    def asked_groups(index, carry):
        for unit in range(UNITS):
            fill(index * UNITS + unit, unit, rows, rows + asked, False)
        for unit in range(UNITS):
            wide = pl.multiple_of((index * UNITS + unit) * lines, lines)
            crossed = product(unit, asked, top * lines)
            folded = sums[pl.ds(wide, lines), :] + fold(crossed, lines, sub_width)
            for m in range(group):
                subspace = unit * group + m
                for half in range(codewords // 128):
                    pieces[2 * (subspace % own) + half, index * share + subspace // own] = folded[
                        m * sub_width : (m + 1) * sub_width, half * 128 : (half + 1) * 128
                    ].astype(BF16)
        for offset in range(1, n_tab):
            copy1(index, tab_peer(offset), my_tab, tab_peer(offset)).start()
        return carry

    lax.fori_loop(0, steps, asked_groups, 0)

    def copy2(source, slot, peer):
        return pltpu.make_async_remote_copy(
            src_ref=middle.at[source], dst_ref=second.at[slot],
            send_sem=sent2.at[source], recv_sem=got2.at[slot],
            device_id=(peer, my_tab), device_id_type=MESH,
        )

    def add1(index, carry):
        rows_here = pl.ds(index * share, share)
        added = pieces[my_tab, rows_here].astype(F32)
        for offset in range(1, n_tab):
            source = tab_peer(n_tab - offset)
            copy1(index, tab_peer(offset), source, tab_peer(offset)).wait_recv()
            added += first[source, rows_here].astype(F32)
        total[rows_here] = added
        middle[rows_here] = added.astype(BF16)
        for number in range(share):
            peer = index * share + number

            @pl.when(peer != my_row)
            def _():
                copy2(peer, my_row, peer).start()

        return carry

    lax.fori_loop(0, steps, add1, 0)

    def add2(offset, held):
        source = row_peer(n_rows - offset)
        copy2(row_peer(offset), source, row_peer(offset)).wait_recv()
        return held + second[source].astype(F32)

    mine[...] = lax.fori_loop(1, n_rows, add2, total[my_row])
    third[my_tab] = mine[...]

    def copy3(slot, peer):
        return pltpu.make_async_remote_copy(
            src_ref=mine, dst_ref=third.at[slot],
            send_sem=sent3.at[peer], recv_sem=got3.at[slot],
            device_id=(my_row, peer), device_id_type=MESH,
        )

    for offset in range(1, n_tab):
        copy3(my_tab, tab_peer(offset)).start()
    pltpu.make_async_remote_copy(
        src_ref=message.at[pl.ds(0, devices - 1)],
        dst_ref=arrived.at[pl.ds(0, devices - 1)],
        send_sem=sent_sem,
        recv_sem=got_sem.at[0],
        device_id=next_door,
        device_id_type=MESH,
    ).wait_send()

    def drain_tab(index, carry):
        for offset in range(1, n_tab):
            copy1(index, tab_peer(offset), my_tab, tab_peer(offset)).wait_send()
        return carry

    def drain_row(offset, carry):
        copy2(row_peer(offset), my_row, row_peer(offset)).wait_send()
        return carry

    lax.fori_loop(0, steps, drain_tab, 0)
    lax.fori_loop(1, n_rows, drain_row, 0)
    for offset in range(1, n_tab):
        copy3(tab_peer(n_tab - offset), tab_peer(offset)).wait_recv()
        copy3(my_tab, tab_peer(offset)).wait_send()
    for half in range(codewords // 128):
        lanes = slice(half * 128, (half + 1) * 128)
        counted = third[2 * own + half]
        for q in range(own):
            weight = counted[q : q + 1] + counted[own + q : own + q + 1] + prior
            out_ref[q, :, lanes] = (third[2 * q + half] + prior * old_ref[q, :, lanes]) / weight


def update(owner, slot, codes_t, old_codebooks, vectors, centroids, rotation, n_rows, n_tab):
    subspaces, rows = codes_t.shape
    lists, width = centroids.shape
    codewords = old_codebooks.shape[2]
    devices = n_rows * n_tab
    asked = 2 * rows
    every = rows + asked
    top = codewords // LOW
    lines = top * (width // subspaces)
    steps = subspaces // (top * UNITS)
    prior = float(rows * devices // codewords)
    vmem, anywhere = pl.BlockSpec(memory_space=pltpu.VMEM), pl.BlockSpec(memory_space=pl.ANY)
    dma = pltpu.SemaphoreType.DMA
    return pl.pallas_call(
        functools.partial(fused_kernel, n_rows, n_tab, prior),
        out_shape=jax.ShapeDtypeStruct(old_codebooks.shape, F32),
        in_specs=[vmem] * 4 + [anywhere] * 3,
        out_specs=vmem,
        scratch_shapes=[
            pltpu.VMEM((rows, width), BF16),
            pltpu.VMEM((lists, width), BF16),
            pltpu.VMEM((width, width), BF16),
            dma((3,)),
            pltpu.VMEM((devices, asked // devices, FIELDS), BF16),
            pltpu.VMEM((devices, asked // devices, FIELDS), BF16),
            dma,
            dma((PLANES // 2,)),
            pltpu.VMEM((width, codewords), F32),
            pltpu.VMEM((subspaces, codewords), F32),
            pltpu.VMEM((width, every), BF16),
            pltpu.VMEM((subspaces, every), F32),
            pltpu.VMEM((subspaces, every), F32),
            pltpu.VMEM((UNITS, top * (lines + top), asked), BF16),
            pltpu.VMEM((UNITS, codewords, asked), BF16),
            pltpu.VMEM((width, lists), BF16),
            pltpu.VMEM((width, width), BF16),
            pltpu.VMEM((n_tab, n_rows, 8, 128), BF16),
            pltpu.VMEM((n_tab, n_rows, 8, 128), BF16),
            pltpu.VMEM((n_rows, 8, 128), F32),
            pltpu.VMEM((n_rows, 8, 128), BF16),
            pltpu.VMEM((n_rows, 8, 128), BF16),
            pltpu.VMEM((8, 128), F32),
            pltpu.VMEM((n_tab, 8, 128), F32),
            dma((steps, n_tab)),
            dma((steps, n_tab)),
            dma((n_rows,)),
            dma((n_rows,)),
            dma((n_tab,)),
            dma((n_tab,)),
        ],
        compiler_params=pltpu.CompilerParams(collective_id=0, has_side_effects=True),
    )(owner, slot, codes_t, old_codebooks, vectors, centroids, rotation)


def body(vectors, list_owner, list_slot, codes, centroids, rotation, old_codebooks):
    row_dev = vectors.shape[0]
    return update(
        list_owner.reshape(1, row_dev),
        list_slot.reshape(1, row_dev),
        codes.T,
        old_codebooks,
        vectors,
        centroids,
        rotation,
        lax.axis_size("rows"),
        lax.axis_size("tab"),
    )


def solution(mesh):
    return jax.shard_map(
        body,
        mesh=mesh,
        in_specs=(
            P(("rows", "tab"), None),
            P(("rows", "tab"), None),
            P(("rows", "tab")),
            P(("rows", "tab"), None),
            P(("rows", "tab"), None),
            P(),
            P("rows", None, None),
        ),
        out_specs=P("rows", None, None),
        check_vma=False,
    )
```

time: 74.1 us -> 58.9 us (0.79)
  Pallas kernels: 71.8 us -> 57.4 us
  other arithmetic: 2.13 us -> 0 us
  local copies, waits for them, and re-layouts: 0.01 us -> 1.35 us
    pallas_call x1, Pallas kernels: 71.8 us -> 57.4 us  [update(): pl.pallas_call(functools.partial(fused_kernel, n_rows, n_tab, prior), out...]
    div x1 -> x0, other arithmetic: 1.36 us -> none  [body(): return (summed[:own] + prior * old_codebooks) / (counts[:, None, :] + prior)]
    unnamed x2 -> x1, local copies, waits for them, and re-layouts: 0.01 us -> 1.35 us
    add x1 -> x0, other arithmetic: 0.78 us -> none  [body(): return (summed[:own] + prior * old_codebooks) / (counts[:, None, :] + prior)]
where the time goes in v4:
time: 58.9 us; the launch traced here: 58.7 us
  Pallas kernels  57.4 us (97%)
  local copies, waits for them, and re-layouts  1.35 us (2%)
    pallas_call x1, Pallas kernels, update(): pl.pallas_call(functools.partial(fused_kernel, n_rows, n_tab, prior), out...  57.4 us
    unnamed x1, local copies, waits for them, and re-layouts  1.35 us

profile of v4, /device:TPU:1, one launch (start us, length us, event | category | flops | bytes accessed | tf_op | source)
XLA Modules:
  0.0 58.7 jit_solution(16787135730892370425)
XLA Ops:
  0.0 57.4 %shard_map.73 = f32[3,8,256]{2,1,0:T(8,128)} custom-call(s32[1,1024]{1,0:T(1,128)} %bitcast.4, s32[1,1024]{1,0:T(1,128)} %bitcast.5, s32[96,1024]{1,0:T(8,128)} %bitcast.3, f32[3,8,256]{2,1,0:T(8,128)} %old_ref.1, bf16[1024,768]{1,0:T(8,128)(2,1)} %vectors_hbm.1, bf16[2048,768]{1,0:T(8,128)(2,1)} %centroids_hbm.1, bf16[768,768]{1,0:T(8,128)(2,1)} %rotation_hbm.1), custom_call_target="tpu_custom_call" | custom-call | tf_op jit(solution)/shard_map/pallas_call | solution.py:369
  57.4 1.3 %copy.9 = f32[3,8,256]{2,1,0:T(8,128)} copy(f32[3,8,256]{2,1,0:T(8,128)} %shard_map.73) | data formatting | bytes 49152
